TPU v7x, 256 devices: a whole 4x4x8 slice. The times are simulated.
256 devices in a mesh: dom: 256 (over y, x, z, core).
Axes of the slice: x: 4, y: 4, z: 8, core: 2. Of those that a mesh axis runs over, the one named last changes fastest.
Arguments:
- embeddings: float32 [131072, 400], P('dom'), may hold values from -1.8 to 1.8
- row_state: float32 [131072], P('dom'), may hold values from 0.01 to 1
- relations: float32 [2048, 400], P('dom'), may hold values from 0.5 to 1.5
- relation_state: float32 [2048], P('dom'), may hold values from 0.01 to 1
- partner_mask: int32 [1], replicated, may hold values from 1 to 255
- source_rows: int32 [786432], P('dom'), may hold values from 0 to 511
- relation_ids: int32 [786432], P('dom'), may hold values from 0 to 2047
- dest_rows: int32 [786432], P('dom'), may hold values from 0 to 511
- negative_rows: int32 [3072, 512], P('dom'), may hold values from 0 to 511
- edge_count: int32 [256], P('dom'), may hold values from 1 to 3072, 491520 in all
Outputs:
- new_embeddings: float32 [131072, 400], P('dom')
- new_row_state: float32 [131072], P('dom')
- new_relations: float32 [2048, 400], P('dom')
- new_relation_state: float32 [2048], P('dom')
Inputs may be any that keep to these rules, and one draw needn't show every extreme that they name: Device i trains the bucket of partition i with partition i XOR partner_mask[0]. `edge_count`: some bucket has all 3072 slots live.
All inputs are finite; a program needn't handle non-finite values. No bound on the sum of `edge_count` on one device may be relied on, other than what follows from the above.
Results may differ from a plain program's by a relative error of at most 0.0015.
Values may be sent and summed in bfloat16 or wider, within the bound.
No kernel may reach another device: no remote copies, remote signals or barrier semaphores. Data moves between devices by JAX's collectives and lax.ppermute only.
A program may use at most 128 MiB of HBM per device.

v0:
```python
import jax
import jax.numpy as jnp
from jax import lax
from jax.sharding import PartitionSpec as P


def from_partner(value, axis, bit):
    mask = 2**bit
    pairs = [(source, source ^ mask) for source in range(lax.axis_size(axis))]
    return lax.ppermute(value, axis, pairs)


def train_bucket(own_bf, part_bf, rel_bf, source, rel_ids, target_rows, negatives, live_count):
    groups, negs_per = negatives.shape
    edges = source.shape[0]
    group_len = edges // groups
    width = own_bf.shape[1]
    own_rows = own_bf[source].astype(jnp.float32)
    rel_rows = rel_bf[rel_ids].astype(jnp.float32)
    queries = (own_rows * rel_rows).astype(jnp.bfloat16)
    target_vals = part_bf[target_rows]
    positive = jnp.sum(queries.astype(jnp.float32) * target_vals.astype(jnp.float32), axis=1)
    sampled = part_bf[negatives]
    grouped = queries.reshape(groups, group_len, width)
    scores = jnp.einsum("gkd,gnd->gkn", grouped, sampled, preferred_element_type=jnp.float32)
    live = (jnp.arange(edges, dtype=jnp.int32) < live_count).astype(jnp.float32)
    pos_grad = -live * jax.nn.sigmoid(-positive)
    neg_grad = (live.reshape(groups, group_len, 1) * jax.nn.sigmoid(scores) / negs_per).astype(
        jnp.bfloat16
    )
    query_grad = pos_grad[:, None] * target_vals.astype(jnp.float32) + jnp.einsum(
        "gkn,gnd->gkd", neg_grad, sampled, preferred_element_type=jnp.float32
    ).reshape(edges, width)
    own_grad = (
        jnp.zeros((own_bf.shape[0], width), jnp.float32).at[source].add(query_grad * rel_rows)
    )
    rel_grad = (
        jnp.zeros((rel_bf.shape[0], width), jnp.float32).at[rel_ids].add(query_grad * own_rows)
    )
    neg_terms = jnp.einsum(
        "gkn,gkd->gnd", neg_grad, grouped, preferred_element_type=jnp.float32
    ).reshape(groups * negs_per, width)
    part_grad = (
        jnp.zeros((part_bf.shape[0], width), jnp.float32)
        .at[target_rows]
        .add(pos_grad[:, None] * queries.astype(jnp.float32))
    )
    part_grad = part_grad.at[negatives.reshape(-1)].add(neg_terms)
    return (own_grad, part_grad.astype(jnp.bfloat16), rel_grad)


def bit_is_set(partner_mask, bit_pos):
    return jnp.bitwise_and(jnp.right_shift(partner_mask[0], bit_pos), 1) == 1


def keep_value(value):
    return value


def swap_forward(bit_pos, value):
    return from_partner(value, "dom", bit_pos)


def swap_back(bit_pos, value):
    return from_partner(value, "dom", bit_pos)


def forward_at(bit_pos):

    def carry_over(value):
        return swap_forward(bit_pos, value)

    return carry_over


def backward_at(bit_pos):

    def carry_back(value):
        return swap_back(bit_pos, value)

    return carry_back


def local(
    embeddings,
    row_state,
    relations,
    relation_state,
    partner_mask,
    source_rows,
    relation_ids,
    dest_rows,
    negative_rows,
    edge_count,
):
    rel_bf = lax.all_gather(relations.astype(jnp.bfloat16), "dom", axis=0, tiled=True)
    own_bf = embeddings.astype(jnp.bfloat16)
    section_count = lax.axis_size("dom").bit_length() - 1
    section_bits = list(range(section_count))
    part_bf = own_bf
    for bit_pos in section_bits:
        part_bf = lax.cond(
            bit_is_set(partner_mask, bit_pos), forward_at(bit_pos), keep_value, part_bf
        )
    own_grad, part_grad, rel_grad = train_bucket(
        own_bf, part_bf, rel_bf, source_rows, relation_ids, dest_rows, negative_rows, edge_count[0]
    )
    returned = part_grad
    for bit_pos in section_bits:
        returned = lax.cond(
            bit_is_set(partner_mask, bit_pos), backward_at(bit_pos), keep_value, returned
        )
    grad = own_grad + returned.astype(jnp.float32)
    new_row_state = row_state + jnp.mean(grad * grad, axis=1)
    new_embeddings = embeddings - 0.1 * grad / jnp.sqrt(new_row_state)[:, None]
    rel_local = relations.shape[0]
    summed = lax.psum(rel_grad, "dom")
    rel_share = lax.dynamic_slice_in_dim(summed, lax.axis_index("dom") * rel_local, rel_local, 0)
    new_relation_state = relation_state + jnp.mean(rel_share * rel_share, axis=1)
    new_relations = relations - 0.1 * rel_share / jnp.sqrt(new_relation_state)[:, None]
    return (new_embeddings, new_row_state, new_relations, new_relation_state)


def solution(mesh):
    in_specs = (
        P("dom", None),
        P("dom"),
        P("dom", None),
        P("dom"),
        P(),
        P("dom"),
        P("dom"),
        P("dom"),
        P("dom", None),
        P("dom"),
    )
    out_specs = (P("dom", None), P("dom"), P("dom", None), P("dom"))
    return jax.shard_map(local, mesh=mesh, in_specs=in_specs, out_specs=out_specs, check_vma=False)
```

profile of v0, /device:TPU:2, one launch (start us, length us, event | category | flops | bytes accessed | tf_op | source)
XLA Modules:
  0.0 463.9 jit_solution(4562606726680797934)
XLA Ops:
  12.5 13.3 %gather_fusion = bf16[3072,400]{1,0:T(8,128)(2,1)} fusion(bf16[512,400]{1,0:T(8,128)(2,1)S(1)} %convert_element_type.144, s32[3072]{0:T(1024)S(1)} %get-tuple-element.107), kind=kCustom, calls=%fused_computation | custom fusion | bytes 4927488 | tf_op jit(solution)/shard_map/gather | solution.py:18
  25.8 27.7 %conditional.18 = (bf16[512,400]{1,0:T(8,128)(2,1)}) conditional(s32[]{:T(128)} %bitcast.5, bf16[512,400]{1,0:T(8,128)(2,1)} %get-tuple-element.111, bf16[512,400]{1,0:T(8,128)(2,1)} %get-tuple-element.111), branch_computations={%region_4.0_spmd, %region_5.0_spmd} | conditional | bytes 2457648 | solution.py:102
  25.9 3.4 collective-permute-start.2
  29.2 23.5 %collective-permute-done.2 = bf16[512,400]{1,0:T(8,128)(2,1)S(1)} collective-permute-done((bf16[512,400]{1,0:T(8,128)(2,1)}, bf16[512,400]{1,0:T(8,128)(2,1)S(1)}, u32[]{:S(2)}, u32[]{:S(2)}) %collective-permute-start.2) | collective-permute-done | bytes 409632 | tf_op jit(solution)/shard_map/cond/branch_1_fun/ppermute | solution.py:10
  53.5 15.6 %conditional.21 = (bf16[512,400]{1,0:T(8,128)(2,1)}) conditional(s32[]{:T(128)} %bitcast.2, bf16[512,400]{1,0:T(8,128)(2,1)} %get-tuple-element.114, bf16[512,400]{1,0:T(8,128)(2,1)} %get-tuple-element.114), branch_computations={%region_10.0_spmd, %region_11.0_spmd} | conditional | bytes 2457648 | solution.py:102
  55.7 12.7 %collective-permute-done.5 = bf16[512,400]{1,0:T(8,128)(2,1)S(1)} collective-permute-done((bf16[512,400]{1,0:T(8,128)(2,1)}, bf16[512,400]{1,0:T(8,128)(2,1)S(1)}, u32[]{:S(2)}, u32[]{:S(2)}) %collective-permute-start.5) | collective-permute-done | bytes 409632 | tf_op jit(solution)/shard_map/cond/branch_1_fun/ppermute | solution.py:10
  69.2 15.1 %conditional.23 = (bf16[512,400]{1,0:T(8,128)(2,1)}) conditional(s32[]{:T(128)} %bitcast, bf16[512,400]{1,0:T(8,128)(2,1)} %get-tuple-element.116, bf16[512,400]{1,0:T(8,128)(2,1)} %get-tuple-element.116), branch_computations={%region_14.0_spmd, %region_15.0_spmd} | conditional | bytes 2457648 | solution.py:102
  72.3 11.1 %collective-permute-done.7 = bf16[512,400]{1,0:T(8,128)(2,1)S(1)} collective-permute-done((bf16[512,400]{1,0:T(8,128)(2,1)}, bf16[512,400]{1,0:T(8,128)(2,1)S(1)}, u32[]{:S(2)}, u32[]{:S(2)}) %collective-permute-start.7) | collective-permute-done | bytes 409632 | tf_op jit(solution)/shard_map/cond/branch_1_fun/ppermute | solution.py:10
  84.3 14.5 %gather_fusion.2 = bf16[3072,400]{1,0:T(8,128)(2,1)} fusion(bf16[512,400]{1,0:T(8,128)(2,1)} %get-tuple-element.117, s32[3072]{0:T(1024)S(1)} %get-tuple-element.108), kind=kCustom, calls=%fused_computation.2 | custom fusion | bytes 4927488 | tf_op jit(solution)/shard_map/gather | solution.py:21
  98.8 26.9 %gather_fusion.3 = bf16[6144,400]{1,0:T(8,128)(2,1)} fusion(bf16[512,400]{1,0:T(8,128)(2,1)} %get-tuple-element.117, s32[6144]{0:T(1024)S(1)} %broadcast_clamp_fusion), kind=kCustom, calls=%fused_computation.3 | custom fusion | bytes 9854976 | tf_op jit(solution)/shard_map/gather | solution.py:23
  129.5 13.0 %gather_fusion.1 = bf16[3072,400]{1,0:T(8,128)(2,1)S(1)} fusion(bf16[2048,400]{1,0:T(8,128)(2,1)} %all-gather.2.cloned.1.call-done, s32[3072]{0:T(1024)S(1)} %get-tuple-element.105), kind=kCustom, calls=%fused_computation.1 | custom fusion | bytes 4927488 | tf_op jit(solution)/shard_map/gather | solution.py:19
  142.6 5.5 %fusion.4 = (f32[3072]{0:T(1024)S(1)}, bf16[3072,400]{1,0:T(8,128)(2,1)S(1)}) fusion(bf16[3072,400]{1,0:T(8,128)(2,1)} %gather_fusion.2, bf16[3072,400]{1,0:T(8,128)(2,1)S(1)} %gather_fusion.1, bf16[3072,400]{1,0:T(8,128)(2,1)} %gather_fusion), kind=kLoop, calls=%fused_computation.18 | loop fusion | flops 9827328 | bytes 9842688 | tf_op jit(solution)/shard_map/reduce_sum | solution.py:22
  157.0 22.0 %scatter_custom_fusion.3 = f32[2048,400]{1,0:T(8,128)} fusion(s32[3072]{0:T(1024)S(1)} %get-tuple-element.104, f32[3072,400]{1,0:T(8,128)} %fusion.5, bf16[3072,400]{1,0:T(8,128)(2,1)S(1)} %copy-done.4, f32[]{:T(128)} %constant.66.clone.1), kind=kCustom, calls=%fused_computation.14 | custom fusion | flops 3686400 | bytes 11337732 | tf_op jit(solution)/shard_map/scatter-add | solution.py:38
  179.1 20.9 %scatter_custom_fusion = f32[512,400]{1,0:T(8,128)S(1)} fusion(s32[3072]{0:T(1024)S(1)} %get-tuple-element.109, bf16[3072,400]{1,0:T(8,128)(2,1)} %copy-done.1, f32[3072]{0:T(1024)S(1)} %divide_multiply_fusion, f32[]{:T(128)} %constant.66.clone.1), kind=kCustom, calls=%fused_computation.17 | custom fusion | flops 3686400 | bytes 3289092 | tf_op jit(solution)/shard_map/scatter-add | solution.py:46
  200.0 9.3 %fusion.13 = f32[12,512,400]{2,1,0:T(8,128)} fusion(bf16[12,256,512]{2,1,0:T(8,128)(2,1)} %copy-done.6, bf16[12,256,400]{2,1,0:T(8,128)(2,1)} %bitcast.31), kind=kOutput, calls=%fused_computation.45 | convolution fusion | flops 1258291200 | bytes 15433728 | tf_op jit(solution)/shard_map/reshape | solution.py:42
  209.3 37.5 %scatter_fusion = f32[512,400]{1,0:T(8,128)S(1)} fusion(f32[512,400]{1,0:T(8,128)S(1)} %scatter_custom_fusion, s32[6144]{0:T(1024)S(1)} %bitcast.34, f32[6144,400]{1,0:T(8,128)} %bitcast.27), kind=kCustom, calls=%fused_computation.5 | custom fusion | flops 2457600 | bytes 29515776 | tf_op jit(solution)/shard_map/scatter-add | solution.py:48
  247.7 28.1 %conditional.26 = (bf16[512,400]{1,0:T(8,128)(2,1)}) conditional(s32[]{:T(128)} %bitcast.5, bf16[512,400]{1,0:T(8,128)(2,1)} %get-tuple-element.119, bf16[512,400]{1,0:T(8,128)(2,1)} %get-tuple-element.119), branch_computations={%region_23.0_spmd, %region_24.0_spmd} | conditional | bytes 2457648 | solution.py:110
  249.7 25.3 %collective-permute-done.10 = bf16[512,400]{1,0:T(8,128)(2,1)S(1)} collective-permute-done((bf16[512,400]{1,0:T(8,128)(2,1)}, bf16[512,400]{1,0:T(8,128)(2,1)S(1)}, u32[]{:S(2)}, u32[]{:S(2)}) %collective-permute-start.10) | collective-permute-done | bytes 409632 | tf_op jit(solution)/shard_map/cond/branch_1_fun/ppermute | solution.py:10
  275.8 15.7 %conditional.29 = (bf16[512,400]{1,0:T(8,128)(2,1)}) conditional(s32[]{:T(128)} %bitcast.2, bf16[512,400]{1,0:T(8,128)(2,1)} %get-tuple-element.122, bf16[512,400]{1,0:T(8,128)(2,1)} %get-tuple-element.122), branch_computations={%region_29.0_spmd, %region_30.0_spmd} | conditional | bytes 2457648 | solution.py:110
  277.9 12.8 %collective-permute-done.13 = bf16[512,400]{1,0:T(8,128)(2,1)S(1)} collective-permute-done((bf16[512,400]{1,0:T(8,128)(2,1)}, bf16[512,400]{1,0:T(8,128)(2,1)S(1)}, u32[]{:S(2)}, u32[]{:S(2)}) %collective-permute-start.13) | collective-permute-done | bytes 409632 | tf_op jit(solution)/shard_map/cond/branch_1_fun/ppermute | solution.py:10
  291.5 15.0 %conditional.31 = (bf16[512,400]{1,0:T(8,128)(2,1)}) conditional(s32[]{:T(128)} %bitcast, bf16[512,400]{1,0:T(8,128)(2,1)} %get-tuple-element.124, bf16[512,400]{1,0:T(8,128)(2,1)} %get-tuple-element.124), branch_computations={%region_33.0_spmd, %region_34.0_spmd} | conditional | bytes 2457648 | solution.py:110
  294.3 11.4 %collective-permute-done.15 = bf16[512,400]{1,0:T(8,128)(2,1)S(1)} collective-permute-done((bf16[512,400]{1,0:T(8,128)(2,1)}, bf16[512,400]{1,0:T(8,128)(2,1)S(1)}, u32[]{:S(2)}, u32[]{:S(2)}) %collective-permute-start.15) | collective-permute-done | bytes 409632 | tf_op jit(solution)/shard_map/cond/branch_1_fun/ppermute | solution.py:10
  308.7 21.9 %scatter_custom_fusion.2 = f32[512,400]{1,0:T(8,128)} fusion(f32[512,400]{1,0:T(8,128)} %convert_element_type.155, s32[3072]{0:T(1024)S(1)} %get-tuple-element.106, f32[3072,400]{1,0:T(8,128)} %fusion.5, bf16[3072,400]{1,0:T(8,128)(2,1)S(1)} %copy-done.3), kind=kCustom, calls=%fused_computation.16 | custom fusion | flops 3686400 | bytes 10256384 | tf_op jit(solution)/shard_map/scatter-add | solution.py:35
  335.5 118.7 %all-reduce.2.cloned.1.call-done = f32[2048,400]{1,0:T(8,128)} async-done(((f32[2048,400]{1,0:T(8,128)}), f32[2048,400]{1,0:T(8,128)}) %all-reduce.2.cloned.1.call-update) | async-done | bytes 3276816 | tf_op jit(solution)/shard_map/psum | solution.py:117
  (80 shorter events, 45.5 us)
Async XLA Ops:
  7.2 122.4 %all-gather.2.cloned.1.call-start = ((), (), s32[]{:S(2)}) async-start(), calls=%async_computation | async-start | bytes 2105344 | tf_op jit(solution)/shard_map/all_gather | solution.py:96
  8.6 445.7 %all-reduce.2.cloned.1.call-start = ((), (), s32[]{:S(2)}) async-start(), calls=%async_computation.1 | async-start | bytes 8388608 | tf_op jit(solution)/shard_map/psum | solution.py:117
  10.7 15.1 %copy-start.7 = (f32[512,400]{1,0:T(8,128)}, f32[512,400]{1,0:T(8,128)S(1)}, u32[]{:S(2)}) copy-start(f32[512,400]{1,0:T(8,128)S(1)} %copy.39) | copy-start | bytes 2457604
  12.5 13.3 %copy-start.8 = (s32[12,512]{1,0:T(8,128)S(1)}, s32[12,512]{1,0:T(8,128)}, u32[]{:S(2)}) copy-start(s32[12,512]{1,0:T(8,128)} %param.50) | copy-start | bytes 73732
  25.8 58.5 %copy-start.10 = (s32[3072]{0:T(1024)S(1)}, s32[3072]{0:T(1024)}, u32[]{:S(2)}) copy-start(s32[3072]{0:T(1024)} %param.49) | copy-start | bytes 36868
  25.9 26.9 %collective-permute-start.2 = (bf16[512,400]{1,0:T(8,128)(2,1)}, bf16[512,400]{1,0:T(8,128)(2,1)S(1)}, u32[]{:S(2)}, u32[]{:S(2)}) collective-permute-start(bf16[512,400]{1,0:T(8,128)(2,1)} %param.5), channel_id=1, source_target_pairs={{0,4},{1,5},{2,6},{3,7},{4,0},{5,1},{6,2},{7,3},{8,12},{9,13},{10,... | collective-permute-start | bytes 1228808 | tf_op jit(solution)/shard_map/cond/branch_1_fun/ppermute | solution.py:10
  53.5 14.8 %collective-permute-start.5 = (bf16[512,400]{1,0:T(8,128)(2,1)}, bf16[512,400]{1,0:T(8,128)(2,1)S(1)}, u32[]{:S(2)}, u32[]{:S(2)}) collective-permute-start(bf16[512,400]{1,0:T(8,128)(2,1)} %param.11), channel_id=1, source_target_pairs={{0,32},{1,33},{2,34},{3,35},{4,36},{5,37},{6,38},{7,39},{8,40},{9,... | collective-permute-start | bytes 1228808 | tf_op jit(solution)/shard_map/cond/branch_1_fun/ppermute | solution.py:10
  69.2 14.3 %collective-permute-start.7 = (bf16[512,400]{1,0:T(8,128)(2,1)}, bf16[512,400]{1,0:T(8,128)(2,1)S(1)}, u32[]{:S(2)}, u32[]{:S(2)}) collective-permute-start(bf16[512,400]{1,0:T(8,128)(2,1)} %param.15), channel_id=1, source_target_pairs={{0,128},{1,129},{2,130},{3,131},{4,132},{5,133},{6,134},{7,135},{8... | collective-permute-start | bytes 1228808 | tf_op jit(solution)/shard_map/cond/branch_1_fun/ppermute | solution.py:10
  98.8 27.6 %copy-start.11 = (s32[3072]{0:T(1024)S(1)}, s32[3072]{0:T(1024)}, u32[]{:S(2)}) copy-start(s32[3072]{0:T(1024)} %param.48) | copy-start | bytes 36868
  142.6 5.5 %copy-start.2 = (bf16[3072,400]{1,0:T(8,128)(2,1)}, bf16[3072,400]{1,0:T(8,128)(2,1)S(1)}, u32[]{:S(2)}) copy-start(bf16[3072,400]{1,0:T(8,128)(2,1)S(1)} %gather_fusion.1) | copy-start | bytes 7372804
  142.6 5.8 %copy-start = (bf16[6144,400]{1,0:T(8,128)(2,1)S(1)}, bf16[6144,400]{1,0:T(8,128)(2,1)}, u32[]{:S(2)}) copy-start(bf16[6144,400]{1,0:T(8,128)(2,1)} %gather_fusion.3) | copy-start | bytes 14745604
  148.1 2.6 copy-start.1
  150.7 1.8 copy-start.6
  150.7 3.0 copy-start.5
  153.8 3.3 copy-start.4
  247.7 61.0 %copy-start.3 = (bf16[3072,400]{1,0:T(8,128)(2,1)S(1)}, bf16[3072,400]{1,0:T(8,128)(2,1)}, u32[]{:S(2)}) copy-start(bf16[3072,400]{1,0:T(8,128)(2,1)} %copy-done.2) | copy-start | bytes 7372804
  247.7 27.3 %collective-permute-start.10 = (bf16[512,400]{1,0:T(8,128)(2,1)}, bf16[512,400]{1,0:T(8,128)(2,1)S(1)}, u32[]{:S(2)}, u32[]{:S(2)}) collective-permute-start(bf16[512,400]{1,0:T(8,128)(2,1)} %param.21), channel_id=1, source_target_pairs={{0,4},{1,5},{2,6},{3,7},{4,0},{5,1},{6,2},{7,3},{8,12},{9,13},{10,... | collective-permute-start | bytes 1228808 | tf_op jit(solution)/shard_map/cond/branch_1_fun/ppermute | solution.py:10
  275.8 14.9 %collective-permute-start.13 = (bf16[512,400]{1,0:T(8,128)(2,1)}, bf16[512,400]{1,0:T(8,128)(2,1)S(1)}, u32[]{:S(2)}, u32[]{:S(2)}) collective-permute-start(bf16[512,400]{1,0:T(8,128)(2,1)} %param.27), channel_id=1, source_target_pairs={{0,32},{1,33},{2,34},{3,35},{4,36},{5,37},{6,38},{7,39},{8,40},{9,... | collective-permute-start | bytes 1228808 | tf_op jit(solution)/shard_map/cond/branch_1_fun/ppermute | solution.py:10
  291.5 14.2 %collective-permute-start.15 = (bf16[512,400]{1,0:T(8,128)(2,1)}, bf16[512,400]{1,0:T(8,128)(2,1)S(1)}, u32[]{:S(2)}, u32[]{:S(2)}) collective-permute-start(bf16[512,400]{1,0:T(8,128)(2,1)} %param.31), channel_id=1, source_target_pairs={{0,128},{1,129},{2,130},{3,131},{4,132},{5,133},{6,134},{7,135},{8... | collective-permute-start | bytes 1228808 | tf_op jit(solution)/shard_map/cond/branch_1_fun/ppermute | solution.py:10
  306.5 25.5 %copy-start.12 = (f32[512]{0:T(512)S(1)}, f32[512]{0:T(512)}, u32[]{:S(2)}) copy-start(f32[512]{0:T(512)} %param.43) | copy-start | bytes 6148
  308.7 146.4 %copy-start.13 = (f32[8]{0:T(128)S(1)}, f32[8]{0:T(128)}, u32[]{:S(2)}) copy-start(f32[8]{0:T(128)} %param.45) | copy-start | bytes 100
  308.7 146.9 %copy-start.9 = (f32[8,400]{1,0:T(8,128)S(1)}, f32[8,400]{1,0:T(8,128)}, u32[]{:S(2)}) copy-start(f32[8,400]{1,0:T(8,128)} %param.44) | copy-start | bytes 38404
Sparse Core Ops, SparseCore 0:
  12.3 117.2 all-gather.1
  179.2 275.0 all-reduce.1
where the time goes:
time: 465 us; the launch traced here: 464 us
  waiting for transfers between devices  219 us (47%)
  other arithmetic  123 us (26%)
  local copies, waits for them, and re-layouts  77.7 us (17%)
  starting transfers between devices  15.7 us (3%)
  between operations  15.6 us (3%)
  matrix products  13.4 us (3%)
    psum x1, waiting for transfers between devices, local(): summed = lax.psum(rel_grad, 'dom')  119 us
    ppermute x6, waiting for transfers between devices, from_partner(): return lax.ppermute(value, axis, pairs)  96.8 us
    scatter-add x1, other arithmetic, train_bucket(): part_grad = part_grad.at[negatives.reshape(-1)].add(neg_terms)  37.5 us
    gather x1, local copies, waits for them, and re-layouts, train_bucket(): sampled = part_bf[negatives]  26.9 us
    scatter-add x1, other arithmetic, train_bucket(): jnp.zeros((rel_bf.shape[0], width), jnp.float32).at[rel_ids]  22 us
    scatter-add x1, other arithmetic, train_bucket(): jnp.zeros((own_bf.shape[0], width), jnp.float32).at[source]  21.9 us
    scatter-add x1, other arithmetic, train_bucket(): part_grad = jnp.zeros((part_bf.shape[0], width), jnp.float32).at[target_r...  20.9 us
    ppermute x6, starting transfers between devices, from_partner(): return lax.ppermute(value, axis, pairs)  15.6 us
  transfers between devices with their start and end apart: 8, of which 8 were waited for; matrix products, arithmetic and copies ran while one was open for 35% of the time, Pallas kernels for 0%

commit v1 on v0

--- a/solution.py
+++ b/solution.py
@@ -93,7 +93,10 @@
     negative_rows,
     edge_count,
 ):
-    rel_bf = lax.all_gather(relations.astype(jnp.bfloat16), "dom", axis=0, tiled=True)
+    a0 = relations.astype(jnp.bfloat16)
+    new = jnp.stack([a0 for _ in range(lax.axis_size("dom"))])
+    d_next = lax.all_to_all(new, "dom", 0, 0)
+    rel_bf = jnp.concatenate(d_next, axis=0)
     own_bf = embeddings.astype(jnp.bfloat16)
     section_count = lax.axis_size("dom").bit_length() - 1
     section_bits = list(range(section_count))

time: 465 us -> 500 us (1.075)
  waiting for transfers between devices: 219 us -> 241 us
  starting transfers between devices: 15.7 us -> 28.2 us
    ppermute x6, waiting for transfers between devices: 96.8 us -> 123 us  [from_partner(): return lax.ppermute(value, axis, pairs)]
    all_to_all x0 -> x1, starting transfers between devices: none -> 14.7 us  [local(): d_next = lax.all_to_all(new, 'dom', 0, 0)]
  transfers between devices with their start and end apart: 8 -> 8, of which waited for: 8 -> 7; matrix products, arithmetic and copies ran while one was open for 35% -> 32% of each run, Pallas kernels for 0% -> 0%
where the time goes in v1:
time: 500 us
  waiting for transfers between devices  241 us (48%)
  other arithmetic  123 us (25%)
  local copies, waits for them, and re-layouts  78.8 us (16%)
  starting transfers between devices  28.2 us (6%)
  between operations  15.6 us (3%)
  matrix products  13.4 us (3%)
    ppermute x6, waiting for transfers between devices, from_partner(): return lax.ppermute(value, axis, pairs)  123 us
    psum x1, waiting for transfers between devices, local(): summed = lax.psum(rel_grad, 'dom')  118 us
    scatter-add x1, other arithmetic, train_bucket(): part_grad = part_grad.at[negatives.reshape(-1)].add(neg_terms)  37.5 us
    gather x1, local copies, waits for them, and re-layouts, train_bucket(): sampled = part_bf[negatives]  26.8 us
    scatter-add x1, other arithmetic, train_bucket(): jnp.zeros((rel_bf.shape[0], width), jnp.float32).at[rel_ids]  22 us
    scatter-add x1, other arithmetic, train_bucket(): jnp.zeros((own_bf.shape[0], width), jnp.float32).at[source]  21.9 us
    scatter-add x1, other arithmetic, train_bucket(): part_grad = jnp.zeros((part_bf.shape[0], width), jnp.float32).at[target_r...  20.9 us
    all_to_all x1, starting transfers between devices, local(): d_next = lax.all_to_all(new, 'dom', 0, 0)  14.7 us
  transfers between devices with their start and end apart: 8, of which 7 were waited for; matrix products, arithmetic and copies ran while one was open for 32% of the time, Pallas kernels for 0%

profile of v1, /device:TPU:2, one launch (start us, length us, event | category | flops | bytes accessed | tf_op | source)
XLA Modules:
  0.0 499.6 jit_solution(1691882036540403006)
XLA Ops:
  9.4 14.7 %all-to-all-start = ((bf16[256,8,400]{2,1,0:T(8,128)(2,1)}), bf16[256,8,400]{2,1,0:T(8,128)(2,1)S(1)}, u32[]{:S(2)}, u32[]{:S(2)}) async-start(bf16[256,8,400]{2,1,0:T(8,128)(2,1)} %stack.2), calls=%async_computation | async-start | bytes 4194304 | tf_op jit(solution)/shard_map/all_to_all | solution.py:98
  28.3 13.3 %gather_fusion = bf16[3072,400]{1,0:T(8,128)(2,1)} fusion(bf16[512,400]{1,0:T(8,128)(2,1)S(1)} %convert_element_type.144, s32[3072]{0:T(1024)S(1)} %get-tuple-element.107), kind=kCustom, calls=%fused_computation | custom fusion | bytes 4927488 | tf_op jit(solution)/shard_map/gather | solution.py:18
  41.6 52.8 %conditional.18 = (bf16[512,400]{1,0:T(8,128)(2,1)}) conditional(s32[]{:T(128)} %bitcast.5, bf16[512,400]{1,0:T(8,128)(2,1)} %get-tuple-element.111, bf16[512,400]{1,0:T(8,128)(2,1)} %get-tuple-element.111), branch_computations={%region_4.0_spmd, %region_5.0_spmd} | conditional | bytes 2457648 | solution.py:105
  44.5 49.1 %collective-permute-done.2 = bf16[512,400]{1,0:T(8,128)(2,1)S(1)} collective-permute-done((bf16[512,400]{1,0:T(8,128)(2,1)}, bf16[512,400]{1,0:T(8,128)(2,1)S(1)}, u32[]{:S(2)}, u32[]{:S(2)}) %collective-permute-start.2) | collective-permute-done | bytes 409632 | tf_op jit(solution)/shard_map/cond/branch_1_fun/ppermute | solution.py:10
  94.4 15.9 %conditional.21 = (bf16[512,400]{1,0:T(8,128)(2,1)}) conditional(s32[]{:T(128)} %bitcast.2, bf16[512,400]{1,0:T(8,128)(2,1)} %get-tuple-element.114, bf16[512,400]{1,0:T(8,128)(2,1)} %get-tuple-element.114), branch_computations={%region_10.0_spmd, %region_11.0_spmd} | conditional | bytes 2457648 | solution.py:105
  96.5 13.0 %collective-permute-done.5 = bf16[512,400]{1,0:T(8,128)(2,1)S(1)} collective-permute-done((bf16[512,400]{1,0:T(8,128)(2,1)}, bf16[512,400]{1,0:T(8,128)(2,1)S(1)}, u32[]{:S(2)}, u32[]{:S(2)}) %collective-permute-start.5) | collective-permute-done | bytes 409632 | tf_op jit(solution)/shard_map/cond/branch_1_fun/ppermute | solution.py:10
  110.3 15.1 %conditional.23 = (bf16[512,400]{1,0:T(8,128)(2,1)}) conditional(s32[]{:T(128)} %bitcast, bf16[512,400]{1,0:T(8,128)(2,1)} %get-tuple-element.116, bf16[512,400]{1,0:T(8,128)(2,1)} %get-tuple-element.116), branch_computations={%region_14.0_spmd, %region_15.0_spmd} | conditional | bytes 2457648 | solution.py:105
  113.4 11.1 %collective-permute-done.7 = bf16[512,400]{1,0:T(8,128)(2,1)S(1)} collective-permute-done((bf16[512,400]{1,0:T(8,128)(2,1)}, bf16[512,400]{1,0:T(8,128)(2,1)S(1)}, u32[]{:S(2)}, u32[]{:S(2)}) %collective-permute-start.7) | collective-permute-done | bytes 409632 | tf_op jit(solution)/shard_map/cond/branch_1_fun/ppermute | solution.py:10
  125.4 14.4 %gather_fusion.2 = bf16[3072,400]{1,0:T(8,128)(2,1)} fusion(bf16[512,400]{1,0:T(8,128)(2,1)} %get-tuple-element.117, s32[3072]{0:T(1024)S(1)} %get-tuple-element.108), kind=kCustom, calls=%fused_computation.2 | custom fusion | bytes 4927488 | tf_op jit(solution)/shard_map/gather | solution.py:21
  139.9 26.8 %gather_fusion.3 = bf16[6144,400]{1,0:T(8,128)(2,1)} fusion(bf16[512,400]{1,0:T(8,128)(2,1)} %get-tuple-element.117, s32[6144]{0:T(1024)S(1)} %broadcast_clamp_fusion), kind=kCustom, calls=%fused_computation.3 | custom fusion | bytes 9854976 | tf_op jit(solution)/shard_map/gather | solution.py:23
  167.4 13.2 %gather_fusion.1 = bf16[3072,400]{1,0:T(8,128)(2,1)} fusion(bf16[2048,400]{1,0:T(8,128)(2,1)S(1)} %bitcast.28, s32[3072]{0:T(1024)S(1)} %get-tuple-element.105), kind=kCustom, calls=%fused_computation.1 | custom fusion | bytes 4927488 | tf_op jit(solution)/shard_map/gather | solution.py:19
  180.6 5.3 %fusion.4 = (f32[3072]{0:T(1024)S(1)}, bf16[3072,400]{1,0:T(8,128)(2,1)S(1)}) fusion(bf16[3072,400]{1,0:T(8,128)(2,1)} %gather_fusion.2, bf16[3072,400]{1,0:T(8,128)(2,1)} %gather_fusion.1, bf16[3072,400]{1,0:T(8,128)(2,1)} %gather_fusion), kind=kLoop, calls=%fused_computation.18 | loop fusion | flops 9827328 | bytes 9842688 | tf_op jit(solution)/shard_map/reduce_sum | solution.py:22
  194.8 22.0 %scatter_custom_fusion.3 = f32[2048,400]{1,0:T(8,128)} fusion(s32[3072]{0:T(1024)S(1)} %get-tuple-element.104, f32[3072,400]{1,0:T(8,128)} %fusion.5, bf16[3072,400]{1,0:T(8,128)(2,1)S(1)} %copy-done.3, f32[]{:T(128)} %constant.66.clone.1), kind=kCustom, calls=%fused_computation.14 | custom fusion | flops 3686400 | bytes 11337732 | tf_op jit(solution)/shard_map/scatter-add | solution.py:38
  216.9 20.9 %scatter_custom_fusion = f32[512,400]{1,0:T(8,128)S(1)} fusion(s32[3072]{0:T(1024)S(1)} %get-tuple-element.109, bf16[3072,400]{1,0:T(8,128)(2,1)} %copy-done.1, f32[3072]{0:T(1024)S(1)} %divide_multiply_fusion, f32[]{:T(128)} %constant.66.clone.1), kind=kCustom, calls=%fused_computation.17 | custom fusion | flops 3686400 | bytes 3289092 | tf_op jit(solution)/shard_map/scatter-add | solution.py:46
  237.8 9.3 %fusion.13 = f32[12,512,400]{2,1,0:T(8,128)} fusion(bf16[12,256,512]{2,1,0:T(8,128)(2,1)} %copy-done.5, bf16[12,256,400]{2,1,0:T(8,128)(2,1)} %bitcast.33), kind=kOutput, calls=%fused_computation.45 | convolution fusion | flops 1258291200 | bytes 15433728 | tf_op jit(solution)/shard_map/reshape | solution.py:42
  247.0 37.5 %scatter_fusion = f32[512,400]{1,0:T(8,128)S(1)} fusion(f32[512,400]{1,0:T(8,128)S(1)} %scatter_custom_fusion, s32[6144]{0:T(1024)S(1)} %bitcast.36, f32[6144,400]{1,0:T(8,128)} %bitcast.29), kind=kCustom, calls=%fused_computation.5 | custom fusion | flops 2457600 | bytes 29515776 | tf_op jit(solution)/shard_map/scatter-add | solution.py:48
  285.5 25.3 %conditional.26 = (bf16[512,400]{1,0:T(8,128)(2,1)}) conditional(s32[]{:T(128)} %bitcast.5, bf16[512,400]{1,0:T(8,128)(2,1)} %get-tuple-element.119, bf16[512,400]{1,0:T(8,128)(2,1)} %get-tuple-element.119), branch_computations={%region_23.0_spmd, %region_24.0_spmd} | conditional | bytes 2457648 | solution.py:113
  285.5 24.5 %collective-permute-done.10 = bf16[512,400]{1,0:T(8,128)(2,1)S(1)} collective-permute-done((bf16[512,400]{1,0:T(8,128)(2,1)}, bf16[512,400]{1,0:T(8,128)(2,1)S(1)}, u32[]{:S(2)}, u32[]{:S(2)}) %collective-permute-start.10) | collective-permute-done | bytes 409632 | tf_op jit(solution)/shard_map/cond/branch_1_fun/ppermute | solution.py:10
  310.8 16.4 %conditional.29 = (bf16[512,400]{1,0:T(8,128)(2,1)}) conditional(s32[]{:T(128)} %bitcast.2, bf16[512,400]{1,0:T(8,128)(2,1)} %get-tuple-element.122, bf16[512,400]{1,0:T(8,128)(2,1)} %get-tuple-element.122), branch_computations={%region_29.0_spmd, %region_30.0_spmd} | conditional | bytes 2457648 | solution.py:113
  313.0 13.4 %collective-permute-done.13 = bf16[512,400]{1,0:T(8,128)(2,1)S(1)} collective-permute-done((bf16[512,400]{1,0:T(8,128)(2,1)}, bf16[512,400]{1,0:T(8,128)(2,1)S(1)}, u32[]{:S(2)}, u32[]{:S(2)}) %collective-permute-start.13) | collective-permute-done | bytes 409632 | tf_op jit(solution)/shard_map/cond/branch_1_fun/ppermute | solution.py:10
  327.1 15.7 %conditional.31 = (bf16[512,400]{1,0:T(8,128)(2,1)}) conditional(s32[]{:T(128)} %bitcast, bf16[512,400]{1,0:T(8,128)(2,1)} %get-tuple-element.124, bf16[512,400]{1,0:T(8,128)(2,1)} %get-tuple-element.124), branch_computations={%region_33.0_spmd, %region_34.0_spmd} | conditional | bytes 2457648 | solution.py:113
  330.3 11.7 %collective-permute-done.15 = bf16[512,400]{1,0:T(8,128)(2,1)S(1)} collective-permute-done((bf16[512,400]{1,0:T(8,128)(2,1)}, bf16[512,400]{1,0:T(8,128)(2,1)S(1)}, u32[]{:S(2)}, u32[]{:S(2)}) %collective-permute-start.15) | collective-permute-done | bytes 409632 | tf_op jit(solution)/shard_map/cond/branch_1_fun/ppermute | solution.py:10
  345.0 21.9 %scatter_custom_fusion.2 = f32[512,400]{1,0:T(8,128)} fusion(f32[512,400]{1,0:T(8,128)} %convert_element_type.155, s32[3072]{0:T(1024)S(1)} %get-tuple-element.106, f32[3072,400]{1,0:T(8,128)} %fusion.5, bf16[3072,400]{1,0:T(8,128)(2,1)S(1)} %copy-done.2), kind=kCustom, calls=%fused_computation.16 | custom fusion | flops 3686400 | bytes 10256384 | tf_op jit(solution)/shard_map/scatter-add | solution.py:35
  371.8 118.1 %all-reduce.2.cloned.1.call-done = f32[2048,400]{1,0:T(8,128)} async-done(((f32[2048,400]{1,0:T(8,128)}), f32[2048,400]{1,0:T(8,128)}) %all-reduce.2.cloned.1.call-update) | async-done | bytes 3276816 | tf_op jit(solution)/shard_map/psum | solution.py:120
  (80 shorter events, 44.5 us)
Async XLA Ops:
  7.2 17.7 %copy-start.6 = (f32[512,400]{0,1:T(8,128)S(1)}, f32[512,400]{0,1:T(8,128)}, u32[]{:S(2)}) copy-start(f32[512,400]{0,1:T(8,128)} %param.42) | copy-start | bytes 2457604
  7.2 21.1 %copy-start.9 = (s32[3072]{0:T(1024)S(1)}, s32[3072]{0:T(1024)}, u32[]{:S(2)}) copy-start(s32[3072]{0:T(1024)} %param.47) | copy-start | bytes 36868
  9.4 157.9 %all-to-all-start = ((bf16[256,8,400]{2,1,0:T(8,128)(2,1)}), bf16[256,8,400]{2,1,0:T(8,128)(2,1)S(1)}, u32[]{:S(2)}, u32[]{:S(2)}) async-start(bf16[256,8,400]{2,1,0:T(8,128)(2,1)} %stack.2), calls=%async_computation | async-start | bytes 4194304 | tf_op jit(solution)/shard_map/all_to_all | solution.py:98
  24.1 465.8 %all-reduce.2.cloned.1.call-start = ((), (), s32[]{:S(2)}) async-start(), calls=%async_computation.1 | async-start | bytes 8388608 | tf_op jit(solution)/shard_map/psum | solution.py:120
  28.3 13.3 %copy-start.7 = (s32[12,512]{1,0:T(8,128)S(1)}, s32[12,512]{1,0:T(8,128)}, u32[]{:S(2)}) copy-start(s32[12,512]{1,0:T(8,128)} %param.50) | copy-start | bytes 73732
  41.6 83.8 %copy-start.10 = (s32[3072]{0:T(1024)S(1)}, s32[3072]{0:T(1024)}, u32[]{:S(2)}) copy-start(s32[3072]{0:T(1024)} %param.49) | copy-start | bytes 36868
  41.6 52.0 %collective-permute-start.2 = (bf16[512,400]{1,0:T(8,128)(2,1)}, bf16[512,400]{1,0:T(8,128)(2,1)S(1)}, u32[]{:S(2)}, u32[]{:S(2)}) collective-permute-start(bf16[512,400]{1,0:T(8,128)(2,1)} %param.5), channel_id=1, source_target_pairs={{0,4},{1,5},{2,6},{3,7},{4,0},{5,1},{6,2},{7,3},{8,12},{9,13},{10,... | collective-permute-start | bytes 1228808 | tf_op jit(solution)/shard_map/cond/branch_1_fun/ppermute | solution.py:10
  94.4 15.1 %collective-permute-start.5 = (bf16[512,400]{1,0:T(8,128)(2,1)}, bf16[512,400]{1,0:T(8,128)(2,1)S(1)}, u32[]{:S(2)}, u32[]{:S(2)}) collective-permute-start(bf16[512,400]{1,0:T(8,128)(2,1)} %param.11), channel_id=1, source_target_pairs={{0,32},{1,33},{2,34},{3,35},{4,36},{5,37},{6,38},{7,39},{8,40},{9,... | collective-permute-start | bytes 1228808 | tf_op jit(solution)/shard_map/cond/branch_1_fun/ppermute | solution.py:10
  110.3 14.2 %collective-permute-start.7 = (bf16[512,400]{1,0:T(8,128)(2,1)}, bf16[512,400]{1,0:T(8,128)(2,1)S(1)}, u32[]{:S(2)}, u32[]{:S(2)}) collective-permute-start(bf16[512,400]{1,0:T(8,128)(2,1)} %param.15), channel_id=1, source_target_pairs={{0,128},{1,129},{2,130},{3,131},{4,132},{5,133},{6,134},{7,135},{8... | collective-permute-start | bytes 1228808 | tf_op jit(solution)/shard_map/cond/branch_1_fun/ppermute | solution.py:10
  139.9 27.5 %copy-start.11 = (s32[3072]{0:T(1024)S(1)}, s32[3072]{0:T(1024)}, u32[]{:S(2)}) copy-start(s32[3072]{0:T(1024)} %param.48) | copy-start | bytes 36868
  180.6 5.5 %copy-start = (bf16[6144,400]{1,0:T(8,128)(2,1)S(1)}, bf16[6144,400]{1,0:T(8,128)(2,1)}, u32[]{:S(2)}) copy-start(bf16[6144,400]{1,0:T(8,128)(2,1)} %gather_fusion.3) | copy-start | bytes 14745604
  185.9 2.5 copy-start.1
  188.5 1.8 copy-start.5
  188.5 3.0 copy-start.4
  191.5 3.3 copy-start.3
  285.4 59.5 %copy-start.2 = (bf16[3072,400]{1,0:T(8,128)(2,1)S(1)}, bf16[3072,400]{1,0:T(8,128)(2,1)}, u32[]{:S(2)}) copy-start(bf16[3072,400]{1,0:T(8,128)(2,1)} %gather_fusion.1) | copy-start | bytes 7372804
  285.5 24.5 %collective-permute-start.10 = (bf16[512,400]{1,0:T(8,128)(2,1)}, bf16[512,400]{1,0:T(8,128)(2,1)S(1)}, u32[]{:S(2)}, u32[]{:S(2)}) collective-permute-start(bf16[512,400]{1,0:T(8,128)(2,1)} %param.21), channel_id=1, source_target_pairs={{0,4},{1,5},{2,6},{3,7},{4,0},{5,1},{6,2},{7,3},{8,12},{9,13},{10,... | collective-permute-start | bytes 1228808 | tf_op jit(solution)/shard_map/cond/branch_1_fun/ppermute | solution.py:10
  310.8 15.6 %collective-permute-start.13 = (bf16[512,400]{1,0:T(8,128)(2,1)}, bf16[512,400]{1,0:T(8,128)(2,1)S(1)}, u32[]{:S(2)}, u32[]{:S(2)}) collective-permute-start(bf16[512,400]{1,0:T(8,128)(2,1)} %param.27), channel_id=1, source_target_pairs={{0,32},{1,33},{2,34},{3,35},{4,36},{5,37},{6,38},{7,39},{8,40},{9,... | collective-permute-start | bytes 1228808 | tf_op jit(solution)/shard_map/cond/branch_1_fun/ppermute | solution.py:10
  327.1 14.9 %collective-permute-start.15 = (bf16[512,400]{1,0:T(8,128)(2,1)}, bf16[512,400]{1,0:T(8,128)(2,1)S(1)}, u32[]{:S(2)}, u32[]{:S(2)}) collective-permute-start(bf16[512,400]{1,0:T(8,128)(2,1)} %param.31), channel_id=1, source_target_pairs={{0,128},{1,129},{2,130},{3,131},{4,132},{5,133},{6,134},{7,135},{8... | collective-permute-start | bytes 1228808 | tf_op jit(solution)/shard_map/cond/branch_1_fun/ppermute | solution.py:10
  342.8 25.5 %copy-start.12 = (f32[512]{0:T(512)S(1)}, f32[512]{0:T(512)}, u32[]{:S(2)}) copy-start(f32[512]{0:T(512)} %param.43) | copy-start | bytes 6148
  345.0 145.8 %copy-start.13 = (f32[8]{0:T(128)S(1)}, f32[8]{0:T(128)}, u32[]{:S(2)}) copy-start(f32[8]{0:T(128)} %param.45) | copy-start | bytes 100
  345.0 146.3 %copy-start.8 = (f32[8,400]{1,0:T(8,128)S(1)}, f32[8,400]{1,0:T(8,128)}, u32[]{:S(2)}) copy-start(f32[8,400]{1,0:T(8,128)} %param.44) | copy-start | bytes 38404
Sparse Core Ops, SparseCore 0:
  216.9 272.9 all-reduce.1
